TPU v7x, 256 devices: a whole 4x4x8 slice. The times are simulated.
256 devices in a mesh: front: 4 (over y_lo, core), blk: 64 (over y_hi, x, z).
Axes of the slice: x: 4, y: 4 (y_hi: 2, y_lo: 2; y = y_hi * 2 + y_lo), z: 8, core: 2. Of those that a mesh axis runs over, the one named last changes fastest.
Arguments:
- front: float32 [4, 8192, 8192], P('front', 'blk'), parts along dimension 0, may hold values from -8 to 40, as said below
- child: float32 [4, 4096, 4096], P('front', 'blk'), parts along dimension 0, may hold values from -1 to 4, as said below
- index_map: int32 [16384], P('front'), parts along dimension 0, may hold values from 0 to 8191, as said below
Outputs:
- factored: float32 [4, 8192, 8192], P('front', 'blk'), parts along dimension 0
There are 4 independent parts, one for each index of `front`. A program takes and returns all parts, laid end to end along the dimension named above; each array names one. Nothing has to cross between parts.
Inputs may be any that keep to these rules, and one draw needn't show every extreme that they name: front is symmetric and positive definite. child is symmetric and positive semidefinite. `index_map`: tile t of the child (indices t * 64 to t * 64 + 63, with t = k * 64 + e and e < 64) maps in increasing order onto 64 different indices of the front's block column b = k * 64 + ((e + h) mod 64), where h is half of 64, that is onto indices b * 128 to b * 128 + 127; no two child indices share a front index.
All inputs are finite; a program needn't handle non-finite values.
Results may differ from a plain program's by a relative error of at most 0.0034.
Values may be sent and summed in bfloat16 or wider, within the bound.
A program may use at most 128 MiB of HBM per device.

v0:
```python
import jax
import jax.numpy as jnp
from jax import lax
from jax.sharding import PartitionSpec as P

PANEL_WIDTH = 512
BLOCK_WIDTH = 128
COL_BLOCKS = 1
TILE_WIDTH = 64
HIGHEST = lax.Precision.HIGHEST


def split_up(shard, dim, count):
    before, after = (shard.shape[:dim], shard.shape[dim + 1 :])
    return jnp.moveaxis(shard.reshape(*before, count, -1, *after), dim, 0)


def sent_and_summed(shard, axis, dim):
    count = lax.axis_size(axis)
    pieces = lax.all_to_all(split_up(shard, dim, count), axis, 0, 0, tiled=True)
    return jnp.sum(pieces, axis=0)


def filled_up(lines, count):
    spare = -lines.shape[0] % count
    if not spare:
        return lines
    return jnp.concatenate([lines, jnp.zeros((spare, *lines.shape[1:]), lines.dtype)])


def from_everyone(shard, axis):
    copies = jnp.broadcast_to(shard, (lax.axis_size(axis), *shard.shape))
    return lax.all_to_all(copies, axis, split_axis=0, concat_axis=0, tiled=True)


def in_order(pieces, dim):
    shape = list(pieces.shape[1:])
    shape[dim] *= pieces.shape[0]
    return jnp.moveaxis(pieces, 0, dim).reshape(shape)


def gathered_copies(shard, axis, dim):
    pieces = from_everyone(shard, axis)
    return in_order(pieces, dim)


def total_of(shard, axes):
    lines = shard.reshape(-1, shard.shape[-1])
    own = sent_and_summed(filled_up(lines, lax.axis_size(axes)), axes, 0)
    whole = gathered_copies(own, axes, 0)
    return whole[: len(lines)].reshape(shard.shape)


def from_behind(shard, axis, by):
    count = lax.axis_size(axis)
    return lax.ppermute(shard, axis, [(i, (i + by) % count) for i in range(count)])


def column_numbers(cycle_size, my_index):
    local_ids = jnp.arange(COL_BLOCKS * BLOCK_WIDTH, dtype=jnp.int32)
    return (
        local_ids // BLOCK_WIDTH * cycle_size + my_index
    ) * BLOCK_WIDTH + local_ids % BLOCK_WIDTH


def row_numbers(cycle_size):
    stored = jnp.arange(cycle_size * COL_BLOCKS * BLOCK_WIDTH, dtype=jnp.int32)
    holder = stored // (COL_BLOCKS * BLOCK_WIDTH)
    within = stored // BLOCK_WIDTH % COL_BLOCKS
    return (within * cycle_size + holder) * BLOCK_WIDTH + stored % BLOCK_WIDTH


def cycle_rows(matrix, cycle_size):
    height = matrix.shape[0]
    return (
        matrix.reshape(height, COL_BLOCKS, cycle_size, BLOCK_WIDTH)
        .transpose(0, 2, 1, 3)
        .reshape(height, -1)
    )


def natural_rows(matrix, cycle_size):
    height = matrix.shape[0]
    return (
        matrix.reshape(height, cycle_size, COL_BLOCKS, BLOCK_WIDTH)
        .transpose(0, 2, 1, 3)
        .reshape(height, -1)
    )


def panel_rows(matrix, row_start, cycle_size):
    first_owner = row_start // BLOCK_WIDTH
    owner_count = PANEL_WIDTH // BLOCK_WIDTH
    height = matrix.shape[0]
    blocks = matrix.reshape(height, cycle_size, COL_BLOCKS, BLOCK_WIDTH)
    return blocks[:, first_owner : first_owner + owner_count, 0, :].reshape(height, PANEL_WIDTH)


def ownership(row_start, my_index):
    first_owner = row_start // BLOCK_WIDTH
    owner_count = PANEL_WIDTH // BLOCK_WIDTH
    is_owner = (my_index >= first_owner) & (my_index < first_owner + owner_count)
    column_start = jnp.clip(my_index - first_owner, 0, owner_count - 1) * BLOCK_WIDTH
    return (is_owner, column_start)


def collect(stacked, row_start, my_index):
    is_owner, column_start = ownership(row_start, my_index)
    padded = jnp.zeros((stacked.shape[0], PANEL_WIDTH, PANEL_WIDTH), jnp.float32)
    padded = lax.dynamic_update_slice(
        padded, jnp.where(is_owner, stacked, 0.0), (0, column_start, 0)
    )
    result = total_of(padded, "blk")
    return result


def own_rows(diag_factor, panel_part, row_start, columns):
    solved = lax.linalg.triangular_solve(
        diag_factor, panel_part, left_side=False, lower=True, transpose_a=True
    )
    offsets = columns - row_start
    diag_rows = jnp.take(diag_factor, jnp.clip(offsets, 0, PANEL_WIDTH - 1), axis=0)
    inside = (offsets >= 0) & (offsets < PANEL_WIDTH)
    before = offsets < 0
    return jnp.where(inside[:, None], diag_rows, jnp.where(before[:, None], 0.0, solved))


def make_refresh(working, lowered, owned_panels, received):
    updated = working - lax.dot_general(
        lowered, received, (((1,), (1,)), ((), ())), preferred_element_type=jnp.float32
    )
    leading = updated
    for is_owner, column_start in owned_panels:
        factor_column = (
            lax.dynamic_slice_in_dim(received, column_start, BLOCK_WIDTH, 1).astype(jnp.float32).T
        )
        leading = jnp.where(is_owner, factor_column, leading)
    return jnp.concatenate([leading, updated[BLOCK_WIDTH:]], axis=0)


def assemble(front, child, index_map, cycle_size, my_index):
    half_cycle = cycle_size // 2
    arrived_tiles = from_behind(child, "blk", half_cycle)
    full_order = 2 * index_map.shape[0]
    tile_places = (index_map % BLOCK_WIDTH).reshape(COL_BLOCKS, cycle_size, TILE_WIDTH)
    places = jnp.arange(BLOCK_WIDTH, dtype=jnp.int32)
    row_table = (tile_places[..., None] == places).astype(jnp.float32)
    shaped = arrived_tiles.reshape(COL_BLOCKS, TILE_WIDTH, COL_BLOCKS, cycle_size, TILE_WIDTH)
    spread = jnp.einsum("acbei,beiq->acbeq", shaped, row_table, precision=HIGHEST)
    spread = jnp.roll(spread, half_cycle, axis=3).reshape(COL_BLOCKS, TILE_WIDTH, full_order)
    source = (my_index - half_cycle) % cycle_size
    own_places = lax.dynamic_index_in_dim(tile_places, source, axis=1, keepdims=False)
    column_table = (own_places[..., None] == places).astype(jnp.float32)
    placed = jnp.einsum("kcq,kcn->kqn", column_table, spread, precision=HIGHEST)
    return front + placed


def on_device(front, child, index_map):
    cycle_size = lax.axis_size("blk")
    my_index = lax.axis_index("blk")
    local_width = COL_BLOCKS * BLOCK_WIDTH
    assembled = assemble(front, child, index_map, cycle_size, my_index).reshape(local_width, -1)
    working = cycle_rows(assembled, cycle_size)
    columns = column_numbers(cycle_size, my_index)
    first_part = panel_rows(working, 0, cycle_size)
    first_diag = collect(first_part[None, :BLOCK_WIDTH], 0, my_index)[0]
    first_rows = own_rows(jnp.linalg.cholesky(first_diag), first_part, 0, columns).astype(
        jnp.bfloat16
    )
    second_part = panel_rows(working, PANEL_WIDTH, cycle_size)
    shared = collect(
        jnp.stack([second_part, first_rows.astype(jnp.float32)]), PANEL_WIDTH, my_index
    )
    crossing = shared[1].astype(jnp.bfloat16)
    second_diag = shared[0] - jnp.dot(crossing, crossing.T, preferred_element_type=jnp.float32)
    second_part = second_part - lax.dot_general(
        first_rows, crossing, (((1,), (1,)), ((), ())), preferred_element_type=jnp.float32
    )
    second_rows = own_rows(
        jnp.linalg.cholesky(second_diag), second_part, PANEL_WIDTH, columns
    ).astype(jnp.bfloat16)
    lowered = jnp.concatenate([first_rows, second_rows], axis=1)
    first_owner = ownership(0, my_index)
    second_owner = ownership(PANEL_WIDTH, my_index)
    owned_panels = (first_owner, (second_owner[0], second_owner[1] + PANEL_WIDTH))
    working = make_refresh(
        working, lowered, owned_panels, lax.all_gather(lowered, "blk", axis=0, tiled=True)
    )
    trailing = columns >= 2 * PANEL_WIDTH
    leading_rows = row_numbers(cycle_size) < 2 * PANEL_WIDTH
    working = jnp.where(trailing[:, None] & leading_rows[None, :], 0.0, working)
    return natural_rows(working, cycle_size).reshape(COL_BLOCKS, BLOCK_WIDTH, -1)


def solution(mesh):
    placed = (P("front", "blk", None), P("front", "blk", None), P("front"))
    return jax.shard_map(
        on_device, mesh=mesh, in_specs=placed, out_specs=P("front", "blk", None), check_vma=False
    )
```

profile of v0, /device:TPU:8, one launch (start us, length us, event | category | flops | bytes accessed | tf_op | source)
XLA Modules:
  0.0 721.6 jit_solution(17179738872541720833)
XLA Ops:
  9.7 23.4 %collective-permute-done = f32[1,64,4096]{2,1,0:T(8,128)S(1)} collective-permute-done((f32[1,64,4096]{2,1,0:T(8,128)}, f32[1,64,4096]{2,1,0:T(8,128)S(1)}, u32[]{:S(2)}, u32[]{:S(2)}) %collective-permute-start) | collective-permute-done | bytes 1048608 | tf_op jit(solution)/shard_map/ppermute | solution.py:56
  45.8 42.7 %all_to_all.20 = f32[64,8,512]{2,1,0:T(8,128)S(1)} all-to-all(f32[64,8,512]{2,1,0:T(8,128)S(1)} %bitcast.161), channel_id=1, replica_groups=mesh['front'=4,'blk'=64] {'blk'}, dimensions={0} | all-to-all | bytes 2097152 | tf_op jit(solution)/shard_map/all_to_all | solution.py:20
  99.1 25.6 %all-to-all-done.1 = f32[64,8,512]{2,1,0:T(8,128)S(1)} async-done(((f32[64,8,512]{2,1,0:T(8,128)}), f32[64,8,512]{2,1,0:T(8,128)S(1)}, u32[]{:S(2)}, u32[]{:S(2)}) %all-to-all-start.1) | async-done | bytes 1048608 | tf_op jit(solution)/shard_map/all_to_all | solution.py:33
  125.3 11.7 %cholesky.286 = f32[128,128]{1,0:T(8,128)S(1)} custom-call(f32[128,128]{1,0:T(8,128)S(1)} %cholesky.426), custom_call_target="Cholesky" | custom-call | tf_op jit(solution)/shard_map/jit(cholesky)/cholesky | solution.py:167
  137.1 9.8 %custom-call.27 = f32[1,128,128]{1,2,0:T(8,128)S(1)} custom-call(f32[1,128,128]{2,1,0:T(8,128)S(1)} %get-tuple-element.74), custom_call_target="InvertDiagBlocksLowerTriangular" | custom-call | tf_op jit(solution)/shard_map/jit(cholesky)/cholesky | solution.py:167
  147.6 11.7 %cholesky.305 = f32[128,128]{1,0:T(8,128)S(1)} custom-call(f32[128,128]{1,0:T(8,128)S(1)} %cholesky.430), custom_call_target="Cholesky" | custom-call | tf_op jit(solution)/shard_map/jit(cholesky)/cholesky | solution.py:167
  159.4 10.0 %custom-call.28 = f32[1,128,128]{1,2,0:T(8,128)S(1)} custom-call(f32[1,128,128]{2,1,0:T(8,128)S(1)} %get-tuple-element.71), custom_call_target="InvertDiagBlocksLowerTriangular" | custom-call | tf_op jit(solution)/shard_map/jit(cholesky)/cholesky | solution.py:167
  170.0 11.7 %cholesky.326 = f32[128,128]{1,0:T(8,128)S(1)} custom-call(f32[128,128]{1,0:T(8,128)S(1)} %cholesky.435), custom_call_target="Cholesky" | custom-call | tf_op jit(solution)/shard_map/jit(cholesky)/cholesky | solution.py:167
  182.5 9.8 %custom-call.29 = f32[1,128,128]{1,2,0:T(8,128)S(1)} custom-call(f32[1,128,128]{2,1,0:T(8,128)S(1)} %get-tuple-element.68), custom_call_target="InvertDiagBlocksLowerTriangular" | custom-call | tf_op jit(solution)/shard_map/jit(cholesky)/cholesky | solution.py:167
  192.9 11.7 %cholesky.343 = f32[128,128]{1,0:T(8,128)S(1)} custom-call(f32[128,128]{1,0:T(8,128)S(1)} %convolution_subtract_fusion.14), custom_call_target="Cholesky" | custom-call | tf_op jit(solution)/shard_map/jit(cholesky)/cholesky | solution.py:167
  216.9 39.3 %custom-call.30 = f32[4,128,128]{1,2,0:T(8,128)S(1)} custom-call(f32[4,128,128]{2,1,0:T(8,128)S(1)} %get-tuple-element.22), custom_call_target="InvertDiagBlocksLowerTriangular" | custom-call | tf_op jit(solution)/shard_map/triangular_solve/custom-call.3 | solution.py:118
  260.2 55.7 %all_to_all.21 = f32[64,16,512]{2,1,0:T(8,128)S(1)} all-to-all(f32[64,16,512]{2,1,0:T(8,128)S(1)} %bitcast.158), channel_id=1, replica_groups=mesh['front'=4,'blk'=64] {'blk'}, dimensions={0} | all-to-all | bytes 4194304 | tf_op jit(solution)/shard_map/all_to_all | solution.py:20
  326.6 47.2 %all-to-all-done.3 = f32[64,16,512]{2,1,0:T(8,128)S(1)} async-done(((f32[64,16,512]{2,1,0:T(8,128)}), f32[64,16,512]{2,1,0:T(8,128)S(1)}, u32[]{:S(2)}, u32[]{:S(2)}) %all-to-all-start.3) | async-done | bytes 2097184 | tf_op jit(solution)/shard_map/all_to_all | solution.py:33
  380.8 11.7 %cholesky.358 = f32[128,128]{1,0:T(8,128)S(1)} custom-call(f32[128,128]{1,0:T(8,128)S(1)} %cholesky.439), custom_call_target="Cholesky" | custom-call | tf_op jit(solution)/shard_map/jit(cholesky)/cholesky | solution.py:180
  392.7 9.8 %custom-call.31 = f32[1,128,128]{1,2,0:T(8,128)S(1)} custom-call(f32[1,128,128]{2,1,0:T(8,128)S(1)} %get-tuple-element.64), custom_call_target="InvertDiagBlocksLowerTriangular" | custom-call | tf_op jit(solution)/shard_map/jit(cholesky)/cholesky | solution.py:180
  405.0 11.7 %cholesky.377 = f32[128,128]{1,0:T(8,128)S(1)} custom-call(f32[128,128]{1,0:T(8,128)S(1)} %cholesky.443), custom_call_target="Cholesky" | custom-call | tf_op jit(solution)/shard_map/jit(cholesky)/cholesky | solution.py:180
  418.1 9.9 %custom-call.32 = f32[1,128,128]{1,2,0:T(8,128)S(1)} custom-call(f32[1,128,128]{2,1,0:T(8,128)S(1)} %get-tuple-element.61), custom_call_target="InvertDiagBlocksLowerTriangular" | custom-call | tf_op jit(solution)/shard_map/jit(cholesky)/cholesky | solution.py:180
  429.6 11.7 %cholesky.398 = f32[128,128]{1,0:T(8,128)S(1)} custom-call(f32[128,128]{1,0:T(8,128)S(1)} %cholesky.448), custom_call_target="Cholesky" | custom-call | tf_op jit(solution)/shard_map/jit(cholesky)/cholesky | solution.py:180
  442.0 9.8 %custom-call.33 = f32[1,128,128]{1,2,0:T(8,128)S(1)} custom-call(f32[1,128,128]{2,1,0:T(8,128)S(1)} %get-tuple-element.58), custom_call_target="InvertDiagBlocksLowerTriangular" | custom-call | tf_op jit(solution)/shard_map/jit(cholesky)/cholesky | solution.py:180
  453.3 11.9 %cholesky.415 = f32[128,128]{1,0:T(8,128)S(1)} custom-call(f32[128,128]{1,0:T(8,128)S(1)} %convolution_subtract_fusion.12), custom_call_target="Cholesky" | custom-call | tf_op jit(solution)/shard_map/jit(cholesky)/cholesky | solution.py:180
  468.7 8.1 %while.5 = (s32[]{:T(128)}, f32[512,512]{1,0:T(8,128)S(1)}, s32[4,2]{0,1:T(2,128)S(1)}, f32[4,128,128]{2,1,0:T(8,128)S(1)}, s32[]{:T(128)}) while((s32[]{:T(128)}, f32[512,512]{1,0:T(8,128)S(1)}, s32[4,2]{0,1:T(2,128)S(1)}, f32[4,128,128]{2,1,0:T(8,128)S(1)}, s32[]{:T(128)}) %tuple.72), condition=%wide.while_cond.clone, body=%wide.while_body.clone.sunk | while | flops 2 | bytes 131181 | solution.py:118
  476.8 39.3 %custom-call.34 = f32[4,128,128]{1,2,0:T(8,128)S(1)} custom-call(f32[4,128,128]{2,1,0:T(8,128)S(1)} %get-tuple-element.23), custom_call_target="InvertDiagBlocksLowerTriangular" | custom-call | tf_op jit(solution)/shard_map/triangular_solve/custom-call.3 | solution.py:118
  520.7 180.0 %all-gather.2.cloned.1.call-done = bf16[8192,1024]{0,1:T(8,128)(2,1)} async-done(((bf16[128,1024]{0,1:T(8,128)(2,1)}), bf16[8192,1024]{0,1:T(8,128)(2,1)}) %all-gather.2.cloned.1.call-update) | async-done | bytes 16777232 | tf_op jit(solution)/shard_map/all_gather | solution.py:187
  700.7 13.8 %fusion.4 = f32[1,128,8192]{2,1,0:T(8,128)} fusion(bf16[8192,1024]{0,1:T(8,128)(2,1)} %all-gather.2.cloned.1.call-done, f32[1,128,8192]{2,1,0:T(8,128)} %copy-done, s32[]{:T(128)S(6)} %select_n.184, s32[]{:T(128)S(6)} %select_n.182, pred[]{:T(512)S(6)} %and.158, pred[]{:T(512)S(6)} %and.156, pred[8192]{0:T(1024)(128)(4,1)S(1)} %fusion.83, ...), kind=kOutput, calls=%fused_computation.12 | convolution fusion | flops 2155347968 | bytes 29630602 | tf_op jit(solution)/shard_map/dot_general | solution.py:129
  (153 shorter events, 90.0 us)
Async XLA Ops:
  6.5 26.6 %collective-permute-start = (f32[1,64,4096]{2,1,0:T(8,128)}, f32[1,64,4096]{2,1,0:T(8,128)S(1)}, u32[]{:S(2)}, u32[]{:S(2)}) collective-permute-start(f32[1,64,4096]{2,1,0:T(8,128)} %param.9), channel_id=1, source_target_pairs={{0,32},{1,33},{2,34},{3,35},{4,36},{5,37},{6,38},{7,39},{8,40},{9,... | collective-permute-start | bytes 3145736 | tf_op jit(solution)/shard_map/ppermute | solution.py:56
  37.9 2.2 copy-start.1
  43.4 2.0 copy-start
  89.7 35.0 %all-to-all-start.1 = ((f32[64,8,512]{2,1,0:T(8,128)}), f32[64,8,512]{2,1,0:T(8,128)S(1)}, u32[]{:S(2)}, u32[]{:S(2)}) async-start(f32[64,8,512]{2,1,0:T(8,128)} %broadcast_in_dim.78), calls=%async_computation.1 | async-start | bytes 2097152 | tf_op jit(solution)/shard_map/all_to_all | solution.py:33
  192.9 63.4 %copy-start.3 = (f32[16,8,4,128]{3,1,2,0:T(8,128)S(1)}, f32[16,8,4,128]{3,1,2,0:T(8,128)}, u32[]{:S(2)}) copy-start(f32[16,8,4,128]{3,1,2,0:T(8,128)} %copy.37) | copy-start | bytes 786436
  208.9 50.7 %copy-start.6 = (pred[128]{0:T(512)(128)(4,1)S(1)}, pred[128]{0:T(512)(128)(4,1)}, u32[]{:S(2)}) copy-start(pred[128]{0:T(512)(128)(4,1)} %get-tuple-element.84) | copy-start | bytes 388
  208.9 50.7 %copy-start.7 = (pred[128]{0:T(512)(128)(4,1)S(1)}, pred[128]{0:T(512)(128)(4,1)}, u32[]{:S(2)}) copy-start(pred[128]{0:T(512)(128)(4,1)} %get-tuple-element.86) | copy-start | bytes 388
  317.7 8.1 %copy-start.8 = (s32[128]{0:T(128)S(1)}, s32[128]{0:T(128)}, u32[]{:S(2)}) copy-start(s32[128]{0:T(128)} %get-tuple-element.79) | copy-start | bytes 1540
  317.7 56.1 %all-to-all-start.3 = ((f32[64,16,512]{2,1,0:T(8,128)}), f32[64,16,512]{2,1,0:T(8,128)S(1)}, u32[]{:S(2)}, u32[]{:S(2)}) async-start(f32[64,16,512]{2,1,0:T(8,128)} %broadcast_in_dim.84), calls=%async_computation.3 | async-start | bytes 4194304 | tf_op jit(solution)/shard_map/all_to_all | solution.py:33
  325.3 375.4 %all-gather.2.cloned.1.call-start = ((), (), s32[]{:S(2)}) async-start(), calls=%async_computation.4 | async-start | bytes 17039360 | tf_op jit(solution)/shard_map/all_gather | solution.py:187
  379.8 1.0 copy-start.2
  452.1 64.1 %copy-start.4 = (f32[128,512]{1,0:T(8,128)S(1)}, f32[128,512]{1,0:T(8,128)}, u32[]{:S(2)}) copy-start(f32[128,512]{1,0:T(8,128)} %copy.23) | copy-start | bytes 786436
  516.2 3.7 copy-start.5
Sparse Core Ops, SparseCore 0:
  520.8 179.8 all-gather.1
where the time goes:
time: 730 us; the launch traced here: 722 us
  waiting for transfers between devices  276 us (38%)
  other arithmetic  241 us (33%)
  blocking collectives  98.4 us (13%)
  matrix products  34.4 us (5%)
  local copies, waits for them, and re-layouts  34.3 us (5%)
  between operations  19.4 us (3%)
  starting transfers between devices  17.2 us (2%)
    all_gather x1, waiting for transfers between devices, on_device(): lax.all_gather(lowered, 'blk', axis=0, tiled=True)  180 us
    all_to_all x2, blocking collectives, sent_and_summed(): pieces = lax.all_to_all(split_up(shard, dim, count), axis, 0, 0, tiled=True)  98.4 us
    another operation x15, other arithmetic, on_device(): jnp.linalg.cholesky(second_diag)  79.4 us
    another operation x5, other arithmetic, own_rows(): lax.linalg.triangular_solve(diag_factor, panel_part, left_side=False, low...  79 us
    another operation x14, other arithmetic, on_device(): jnp.linalg.cholesky(first_diag)  78.8 us
    all_to_all x2, waiting for transfers between devices, from_everyone(): return lax.all_to_all(copies, axis, split_axis=0, concat_axis=0, tiled=True)  72.8 us
    ppermute x1, waiting for transfers between devices, from_behind(): lax.ppermute(shard, axis, [(i, (i + by) % count) for i in range(count)])  23.4 us
    another operation x27, local copies, waits for them, and re-layouts, own_rows(): lax.linalg.triangular_solve(diag_factor, panel_part, left_side=False, low...  16 us
  transfers between devices with their start and end apart: 4, of which 4 were waited for; matrix products, arithmetic and copies ran while one was open for 1% of the time, Pallas kernels for 0%

commit v1 on v0

--- a/solution.py
+++ b/solution.py
@@ -8,6 +8,11 @@
 COL_BLOCKS = 1
 TILE_WIDTH = 64
 HIGHEST = lax.Precision.HIGHEST
+
+
+def all_by_exchange(block, axis, d):
+    sent = jnp.stack([block] * lax.axis_size(axis))
+    return jnp.concatenate(lax.all_to_all(sent, axis, 0, 0), axis=d)
 
 
 def split_up(shard, dim, count):
@@ -183,9 +188,7 @@
     first_owner = ownership(0, my_index)
     second_owner = ownership(PANEL_WIDTH, my_index)
     owned_panels = (first_owner, (second_owner[0], second_owner[1] + PANEL_WIDTH))
-    working = make_refresh(
-        working, lowered, owned_panels, lax.all_gather(lowered, "blk", axis=0, tiled=True)
-    )
+    working = make_refresh(working, lowered, owned_panels, all_by_exchange(lowered, "blk", 0))
     trailing = columns >= 2 * PANEL_WIDTH
     leading_rows = row_numbers(cycle_size) < 2 * PANEL_WIDTH
     working = jnp.where(trailing[:, None] & leading_rows[None, :], 0.0, working)

time: 730 us -> 922 us (1.26)
  the two profiles are of different devices: /device:TPU:8 before, /device:TPU:36 now
where the time goes in v1:
time: 922 us; the launch traced here: 914 us
  waiting for transfers between devices  466 us (51%)
  other arithmetic  241 us (26%)
  blocking collectives  99.3 us (11%)
  local copies, waits for them, and re-layouts  49.3 us (5%)
  matrix products  26.8 us (3%)
  starting transfers between devices  25.5 us (3%)
    all_to_all x1, waiting for transfers between devices, all_by_exchange(): return jnp.concatenate(lax.all_to_all(sent, axis, 0, 0), axis=d)  371 us
    all_to_all x2, blocking collectives, sent_and_summed(): pieces = lax.all_to_all(split_up(shard, dim, count), axis, 0, 0, tiled=True)  99.3 us
    another operation x15, other arithmetic, on_device(): jnp.linalg.cholesky(second_diag)  79.4 us
    another operation x5, other arithmetic, own_rows(): lax.linalg.triangular_solve(diag_factor, panel_part, left_side=False, low...  79 us
    another operation x14, other arithmetic, on_device(): jnp.linalg.cholesky(first_diag)  78.8 us
    all_to_all x2, waiting for transfers between devices, from_everyone(): return lax.all_to_all(copies, axis, split_axis=0, concat_axis=0, tiled=True)  72.5 us
    ppermute x1, waiting for transfers between devices, from_behind(): lax.ppermute(shard, axis, [(i, (i + by) % count) for i in range(count)])  22.5 us
  transfers between devices with their start and end apart: 4, of which 4 were waited for; matrix products, arithmetic and copies ran while one was open for 0% of the time, Pallas kernels for 0%

profile of v1, /device:TPU:36, one launch (start us, length us, event | category | flops | bytes accessed | tf_op | source)
XLA Modules:
  0.0 913.6 jit_solution(9900221301815594237)
XLA Ops:
  4.1 22.5 %collective-permute-done = f32[1,64,4096]{2,1,0:T(8,128)S(1)} collective-permute-done((f32[1,64,4096]{2,1,0:T(8,128)}, f32[1,64,4096]{2,1,0:T(8,128)S(1)}, u32[]{:S(2)}, u32[]{:S(2)}) %collective-permute-start) | collective-permute-done | bytes 1048608 | tf_op jit(solution)/shard_map/ppermute | solution.py:61
  39.4 42.6 %all_to_all.25 = f32[64,8,512]{2,1,0:T(8,128)S(1)} all-to-all(f32[64,8,512]{2,1,0:T(8,128)S(1)} %bitcast.170), channel_id=1, replica_groups=mesh['front'=4,'blk'=64] {'blk'}, dimensions={0} | all-to-all | bytes 2097152 | tf_op jit(solution)/shard_map/all_to_all | solution.py:25
  94.0 24.0 %all-to-all-done.1 = f32[64,8,512]{2,1,0:T(8,128)S(1)} async-done(((f32[64,8,512]{2,1,0:T(8,128)}), f32[64,8,512]{2,1,0:T(8,128)S(1)}, u32[]{:S(2)}, u32[]{:S(2)}) %all-to-all-start.1) | async-done | bytes 1048608 | tf_op jit(solution)/shard_map/all_to_all | solution.py:38
  118.6 11.7 %cholesky.286 = f32[128,128]{1,0:T(8,128)S(1)} custom-call(f32[128,128]{1,0:T(8,128)S(1)} %cholesky.426), custom_call_target="Cholesky" | custom-call | tf_op jit(solution)/shard_map/jit(cholesky)/cholesky | solution.py:172
  130.5 9.8 %custom-call.27 = f32[1,128,128]{1,2,0:T(8,128)S(1)} custom-call(f32[1,128,128]{2,1,0:T(8,128)S(1)} %get-tuple-element.74), custom_call_target="InvertDiagBlocksLowerTriangular" | custom-call | tf_op jit(solution)/shard_map/jit(cholesky)/cholesky | solution.py:172
  141.0 11.7 %cholesky.305 = f32[128,128]{1,0:T(8,128)S(1)} custom-call(f32[128,128]{1,0:T(8,128)S(1)} %cholesky.430), custom_call_target="Cholesky" | custom-call | tf_op jit(solution)/shard_map/jit(cholesky)/cholesky | solution.py:172
  152.7 9.9 %custom-call.28 = f32[1,128,128]{1,2,0:T(8,128)S(1)} custom-call(f32[1,128,128]{2,1,0:T(8,128)S(1)} %get-tuple-element.71), custom_call_target="InvertDiagBlocksLowerTriangular" | custom-call | tf_op jit(solution)/shard_map/jit(cholesky)/cholesky | solution.py:172
  163.4 11.7 %cholesky.326 = f32[128,128]{1,0:T(8,128)S(1)} custom-call(f32[128,128]{1,0:T(8,128)S(1)} %cholesky.435), custom_call_target="Cholesky" | custom-call | tf_op jit(solution)/shard_map/jit(cholesky)/cholesky | solution.py:172
  175.8 9.8 %custom-call.29 = f32[1,128,128]{1,2,0:T(8,128)S(1)} custom-call(f32[1,128,128]{2,1,0:T(8,128)S(1)} %get-tuple-element.68), custom_call_target="InvertDiagBlocksLowerTriangular" | custom-call | tf_op jit(solution)/shard_map/jit(cholesky)/cholesky | solution.py:172
  186.2 11.7 %cholesky.343 = f32[128,128]{1,0:T(8,128)S(1)} custom-call(f32[128,128]{1,0:T(8,128)S(1)} %convolution_subtract_fusion.14), custom_call_target="Cholesky" | custom-call | tf_op jit(solution)/shard_map/jit(cholesky)/cholesky | solution.py:172
  210.0 39.3 %custom-call.30 = f32[4,128,128]{1,2,0:T(8,128)S(1)} custom-call(f32[4,128,128]{2,1,0:T(8,128)S(1)} %get-tuple-element.22), custom_call_target="InvertDiagBlocksLowerTriangular" | custom-call | tf_op jit(solution)/shard_map/triangular_solve/custom-call.3 | solution.py:123
  253.4 56.7 %all_to_all.26 = f32[64,16,512]{2,1,0:T(8,128)S(1)} all-to-all(f32[64,16,512]{2,1,0:T(8,128)S(1)} %bitcast.167), channel_id=1, replica_groups=mesh['front'=4,'blk'=64] {'blk'}, dimensions={0} | all-to-all | bytes 4194304 | tf_op jit(solution)/shard_map/all_to_all | solution.py:25
  319.4 48.5 %all-to-all-done.3 = f32[64,16,512]{2,1,0:T(8,128)S(1)} async-done(((f32[64,16,512]{2,1,0:T(8,128)}), f32[64,16,512]{2,1,0:T(8,128)S(1)}, u32[]{:S(2)}, u32[]{:S(2)}) %all-to-all-start.3) | async-done | bytes 2097184 | tf_op jit(solution)/shard_map/all_to_all | solution.py:38
  374.9 11.7 %cholesky.358 = f32[128,128]{1,0:T(8,128)S(1)} custom-call(f32[128,128]{1,0:T(8,128)S(1)} %cholesky.439), custom_call_target="Cholesky" | custom-call | tf_op jit(solution)/shard_map/jit(cholesky)/cholesky | solution.py:185
  386.8 9.8 %custom-call.31 = f32[1,128,128]{1,2,0:T(8,128)S(1)} custom-call(f32[1,128,128]{2,1,0:T(8,128)S(1)} %get-tuple-element.64), custom_call_target="InvertDiagBlocksLowerTriangular" | custom-call | tf_op jit(solution)/shard_map/jit(cholesky)/cholesky | solution.py:185
  399.1 11.7 %cholesky.377 = f32[128,128]{1,0:T(8,128)S(1)} custom-call(f32[128,128]{1,0:T(8,128)S(1)} %cholesky.443), custom_call_target="Cholesky" | custom-call | tf_op jit(solution)/shard_map/jit(cholesky)/cholesky | solution.py:185
  412.3 9.9 %custom-call.32 = f32[1,128,128]{1,2,0:T(8,128)S(1)} custom-call(f32[1,128,128]{2,1,0:T(8,128)S(1)} %get-tuple-element.61), custom_call_target="InvertDiagBlocksLowerTriangular" | custom-call | tf_op jit(solution)/shard_map/jit(cholesky)/cholesky | solution.py:185
  423.8 11.7 %cholesky.398 = f32[128,128]{1,0:T(8,128)S(1)} custom-call(f32[128,128]{1,0:T(8,128)S(1)} %cholesky.448), custom_call_target="Cholesky" | custom-call | tf_op jit(solution)/shard_map/jit(cholesky)/cholesky | solution.py:185
  436.2 9.8 %custom-call.33 = f32[1,128,128]{1,2,0:T(8,128)S(1)} custom-call(f32[1,128,128]{2,1,0:T(8,128)S(1)} %get-tuple-element.58), custom_call_target="InvertDiagBlocksLowerTriangular" | custom-call | tf_op jit(solution)/shard_map/jit(cholesky)/cholesky | solution.py:185
  447.4 11.9 %cholesky.415 = f32[128,128]{1,0:T(8,128)S(1)} custom-call(f32[128,128]{1,0:T(8,128)S(1)} %convolution_subtract_fusion.12), custom_call_target="Cholesky" | custom-call | tf_op jit(solution)/shard_map/jit(cholesky)/cholesky | solution.py:185
  462.7 8.3 while.5
  471.1 39.3 %custom-call.34 = f32[4,128,128]{1,2,0:T(8,128)S(1)} custom-call(f32[4,128,128]{2,1,0:T(8,128)S(1)} %get-tuple-element.23), custom_call_target="InvertDiagBlocksLowerTriangular" | custom-call | tf_op jit(solution)/shard_map/triangular_solve/custom-call.3 | solution.py:123
  527.6 370.7 %all-to-all-done.4 = bf16[64,128,1024]{1,2,0:T(8,128)(2,1)} async-done(((bf16[64,128,1024]{1,2,0:T(8,128)(2,1)}), bf16[64,128,1024]{1,2,0:T(8,128)(2,1)}, u32[]{:S(2)}, u32[]{:S(2)}) %all-to-all-start.4) | async-done | bytes 16777248 | tf_op jit(solution)/shard_map/all_to_all | solution.py:15
  898.4 9.0 copy_bitcast_fusion
  (155 shorter events, 109.6 us)
Async XLA Ops:
  0.0 26.6 %collective-permute-start = (f32[1,64,4096]{2,1,0:T(8,128)}, f32[1,64,4096]{2,1,0:T(8,128)S(1)}, u32[]{:S(2)}, u32[]{:S(2)}) collective-permute-start(f32[1,64,4096]{2,1,0:T(8,128)} %param.9), channel_id=1, source_target_pairs={{0,32},{1,33},{2,34},{3,35},{4,36},{5,37},{6,38},{7,39},{8,40},{9,... | collective-permute-start | bytes 3145736 | tf_op jit(solution)/shard_map/ppermute | solution.py:61
  31.3 2.2 copy-start.2
  37.0 2.0 copy-start
  83.1 34.9 %all-to-all-start.1 = ((f32[64,8,512]{2,1,0:T(8,128)}), f32[64,8,512]{2,1,0:T(8,128)S(1)}, u32[]{:S(2)}, u32[]{:S(2)}) async-start(f32[64,8,512]{2,1,0:T(8,128)} %broadcast_in_dim.78), calls=%async_computation.1 | async-start | bytes 2097152 | tf_op jit(solution)/shard_map/all_to_all | solution.py:38
  186.2 63.1 %copy-start.5 = (f32[16,8,4,128]{3,1,2,0:T(8,128)S(1)}, f32[16,8,4,128]{3,1,2,0:T(8,128)}, u32[]{:S(2)}) copy-start(f32[16,8,4,128]{3,1,2,0:T(8,128)} %copy.48) | copy-start | bytes 786436
  202.2 50.5 %copy-start.7 = (pred[128]{0:T(512)(128)(4,1)S(1)}, pred[128]{0:T(512)(128)(4,1)}, u32[]{:S(2)}) copy-start(pred[128]{0:T(512)(128)(4,1)} %get-tuple-element.84) | copy-start | bytes 388
  202.2 50.5 %copy-start.8 = (pred[128]{0:T(512)(128)(4,1)S(1)}, pred[128]{0:T(512)(128)(4,1)}, u32[]{:S(2)}) copy-start(pred[128]{0:T(512)(128)(4,1)} %get-tuple-element.86) | copy-start | bytes 388
  210.0 42.8 %copy-start.4 = (f32[128,4,1,128]{0,3,1,2:T(8,128)S(1)}, f32[128,4,1,128]{0,3,1,2:T(8,128)}, u32[]{:S(2)}) copy-start(f32[128,4,1,128]{0,3,1,2:T(8,128)} %copy.24) | copy-start | bytes 786436
  311.8 7.6 copy-start.9
  311.8 56.1 %all-to-all-start.3 = ((f32[64,16,512]{2,1,0:T(8,128)}), f32[64,16,512]{2,1,0:T(8,128)S(1)}, u32[]{:S(2)}, u32[]{:S(2)}) async-start(f32[64,16,512]{2,1,0:T(8,128)} %broadcast_in_dim.84), calls=%async_computation.3 | async-start | bytes 4194304 | tf_op jit(solution)/shard_map/all_to_all | solution.py:38
  373.9 1.0 copy-start.3
  510.4 3.7 copy-start.6
  520.4 378.0 %all-to-all-start.4 = ((bf16[64,128,1024]{1,2,0:T(8,128)(2,1)}), bf16[64,128,1024]{1,2,0:T(8,128)(2,1)}, u32[]{:S(2)}, u32[]{:S(2)}) async-start(bf16[64,128,1024]{1,2,0:T(8,128)(2,1)} %stack.12), calls=%async_computation.4 | async-start | bytes 33554432 | tf_op jit(solution)/shard_map/all_to_all | solution.py:15
  898.4 9.0 copy-start.1
